TPU v7x, 128 devices: a whole 4x4x4 slice. The times are simulated.
128 devices in a mesh: dp: 16 (over x, y_hi, core), code: 8 (over y_lo, z).
Axes of the slice: x: 4, y: 4 (y_hi: 2, y_lo: 2; y = y_hi * 2 + y_lo), z: 4, core: 2. Of those that a mesh axis runs over, the one named last changes fastest.
Arguments:
- temporal_out: bfloat16 [2048, 4096], P('dp'), may hold values from -6 to 6
- depth_in: bfloat16 [8, 4096, 1024], P('code', 'dp'), may hold values from -0.09375 to 0.09375
- embed: bfloat16 [8, 1024, 1024], P('code'), may hold values from -6 to 6
- depth_w1: bfloat16 [8, 1024, 2112], P('code', None, 'dp'), may hold values from -0.1875 to 0.1875
- depth_w2: bfloat16 [8, 1024, 2112], P('code', None, 'dp'), may hold values from -0.125 to 0.125
- audio_tokens: int32 [2048, 8], P(None, 'code'), may hold values from 0 to 1023
- barge_mask: int32 [2048], P('dp'), may hold values 0 or 1
- out_grad: bfloat16 [2048, 8, 1024], P('dp', 'code'), may hold values from -6 to 6
Outputs:
- temporal_grad: bfloat16 [2048, 4096], P('dp', 'code')
- depth_in_grad: bfloat16 [8, 4096, 1024], P('code', 'dp')
- embed_grad: bfloat16 [8, 1024, 1024], P('code', 'dp')
- w1_grad: bfloat16 [8, 1024, 2112], P('code', None, 'dp')
- w2_grad: bfloat16 [8, 1024, 2112], P('code', None, 'dp')
All inputs are finite; a program needn't handle non-finite values. No bound on the sum of `barge_mask` on one device may be relied on, other than what follows from the above.
Results may differ from a plain program's by a relative error of at most 0.02.
Values may be sent and summed in bfloat16 or wider, within the bound.
No kernel may reach another device: no remote copies, remote signals or barrier semaphores. Data moves between devices by JAX's collectives and lax.ppermute only.
A program may use at most 128 MiB of HBM per device.

v0:
```python
import jax
import jax.numpy as jnp
from jax import lax
from jax.sharding import PartitionSpec as P

EPS = 1e-06


def shifted(block, axis, distance):
    devices = range(lax.axis_size(axis))
    route = [(i - distance, i) for i in devices if i - distance in devices]
    return lax.ppermute(block, axis, route)


def matmul(left, right):
    return jnp.dot(left, right, preferred_element_type=jnp.float32)


def contract_rows(left, right):
    return lax.dot_general(
        left, right, (((0,), (0,)), ((), ())), preferred_element_type=jnp.float32
    )


def contract_cols(left, right):
    return lax.dot_general(
        left, right, (((1,), (1,)), ((), ())), preferred_element_type=jnp.float32
    )


def silu_slope(values):
    sigma = jax.nn.sigmoid(values)
    return sigma * (1.0 + values * (1.0 - sigma))


def per_device(
    temporal_out, depth_in, embed, depth_w1, depth_w2, audio_tokens, barge_mask, out_grad
):
    dp_index = lax.axis_index("dp")
    n_code = lax.axis_size("code")
    own_rows = temporal_out.shape[0]
    projection = lax.all_gather(depth_in[0], "dp", axis=0, tiled=True)
    table = embed[0]
    token_all = audio_tokens[:, 0]
    token_own = lax.dynamic_slice_in_dim(token_all, dp_index * own_rows, own_rows, 0)
    depth_base = matmul(temporal_out, projection) + jnp.take(table, token_own, axis=0).astype(
        jnp.float32
    )
    width_depth = depth_base.shape[1]
    w_first, w_second = (
        lax.all_gather(depth_w1[0], "dp", axis=1, tiled=True),
        lax.all_gather(depth_w2[0], "dp", axis=1, tiled=True),
    )

    def depth_hidden(resid):
        scale = lax.rsqrt(jnp.mean(resid * resid, axis=-1, keepdims=True) + EPS)
        normed = (resid * scale).astype(jnp.bfloat16)
        pre_act = matmul(normed, w_first)
        active = jax.nn.silu(pre_act).astype(jnp.bfloat16)
        return (scale, normed, pre_act, active)

    def forward_turn(turn_index, incoming):
        resid = depth_base + incoming.astype(jnp.float32)
        scale, normed, pre_act, active = depth_hidden(resid)
        state = (resid + contract_cols(active, w_second)).astype(jnp.bfloat16)
        return shifted(state, "code", 1)

    start_state = jnp.zeros((own_rows, width_depth), jnp.bfloat16)
    incoming = lax.fori_loop(0, n_code - 1, forward_turn, start_state)
    resid = depth_base + incoming.astype(jnp.float32)
    scale, normed, pre_act, active = depth_hidden(resid)
    unit_rows = resid * scale
    derivative = silu_slope(pre_act)
    cotangent = out_grad[:, 0, :].astype(jnp.float32) * barge_mask.astype(jnp.float32)[:, None]

    def depth_back(from_next):
        state_slope = cotangent + from_next.astype(jnp.float32)
        slope_b = state_slope.astype(jnp.bfloat16)
        pre_slope = (matmul(slope_b, w_second) * derivative).astype(jnp.bfloat16)
        norm_slope = contract_cols(pre_slope, w_first)
        carried = (
            state_slope
            + scale
            * (norm_slope - unit_rows * jnp.mean(norm_slope * unit_rows, axis=-1, keepdims=True))
        ).astype(jnp.bfloat16)
        return (carried, slope_b, pre_slope)

    def backward_turn(turn_index, from_next):
        return shifted(depth_back(from_next)[0], "code", -1)

    from_next = lax.fori_loop(0, n_code - 1, backward_turn, start_state)
    carried, slope_b, pre_slope = depth_back(from_next)
    first_grad, second_grad = (
        lax.psum_scatter(
            contract_rows(normed, pre_slope).astype(jnp.bfloat16),
            "dp",
            scatter_dimension=1,
            tiled=True,
        ).astype(jnp.float32),
        lax.psum_scatter(
            contract_rows(slope_b, active).astype(jnp.bfloat16),
            "dp",
            scatter_dimension=1,
            tiled=True,
        ).astype(jnp.float32),
    )
    temporal_grad = lax.psum_scatter(
        contract_cols(carried, projection).astype(jnp.bfloat16),
        "code",
        scatter_dimension=1,
        tiled=True,
    )
    vocab_ids = lax.broadcasted_iota(jnp.int32, (1, table.shape[0]), 1)
    onehot = (token_own[:, None] == vocab_ids).astype(jnp.bfloat16)
    proj_grad, table_grad = (
        lax.psum_scatter(
            contract_rows(temporal_out, carried).astype(jnp.bfloat16),
            "dp",
            scatter_dimension=0,
            tiled=True,
        ).astype(jnp.float32),
        lax.psum_scatter(
            contract_rows(onehot, carried).astype(jnp.bfloat16),
            "dp",
            scatter_dimension=0,
            tiled=True,
        ).astype(jnp.float32),
    )
    return (
        temporal_grad,
        proj_grad.astype(jnp.bfloat16)[None],
        table_grad.astype(jnp.bfloat16)[None],
        first_grad.astype(jnp.bfloat16)[None],
        second_grad.astype(jnp.bfloat16)[None],
    )


def solution(mesh):
    in_specs = (
        P("dp", None),
        P("code", "dp", None),
        P("code", None, None),
        P("code", None, "dp"),
        P("code", None, "dp"),
        P(None, "code"),
        P("dp"),
        P("dp", "code", None),
    )
    out_specs = (
        P("dp", "code"),
        P("code", "dp", None),
        P("code", "dp", None),
        P("code", None, "dp"),
        P("code", None, "dp"),
    )
    return jax.shard_map(
        per_device, mesh=mesh, in_specs=in_specs, out_specs=out_specs, check_vma=False
    )
```

profile of v0, /device:TPU:0, one launch (start us, length us, event | category | flops | bytes accessed | tf_op | source)
XLA Modules:
  0.0 786.8 jit_solution(18314862474826231828)
XLA Ops:
  15.0 71.7 %all-gather.9.cloned.1.call-done = bf16[1,1024,2112]{1,0,2:T(2,128)(2,1)} async-done(((bf16[1,1024,132]{1,0,2:T(2,128)(2,1)}), bf16[1,1024,2112]{1,0,2:T(2,128)(2,1)}) %all-gather.9.cloned.1.call-update) | async-done | bytes 4325392 | tf_op jit(solution)/shard_map/all_gather | solution.py:51
  86.7 20.8 %copy.34 = bf16[1,1024,2112]{2,1,0:T(8,128)(2,1)} copy(bf16[1,1024,2112]{1,0,2:T(2,128)(2,1)} %all-gather.9.cloned.1.call-done) | data formatting | bytes 8650752
  107.5 53.2 %all-gather.11.cloned.1.call-done = bf16[1,1024,2112]{1,0,2:T(2,128)(2,1)} async-done(((bf16[1,1024,132]{1,0,2:T(2,128)(2,1)}), bf16[1,1024,2112]{1,0,2:T(2,128)(2,1)}) %all-gather.11.cloned.1.call-update) | async-done | bytes 4325392 | tf_op jit(solution)/shard_map/all_gather | solution.py:52
  160.8 20.9 %copy.35 = bf16[1,1024,2112]{2,1,0:T(8,128)(2,1)} copy(bf16[1,1024,2112]{1,0,2:T(2,128)(2,1)} %all-gather.11.cloned.1.call-done) | data formatting | bytes 8650752
  181.7 52.1 %all-gather.7.cloned.1.call-done = bf16[1,4096,1024]{2,1,0:T(8,128)(2,1)} async-done(((bf16[1,256,1024]{2,1,0:T(8,128)(2,1)}), bf16[1,4096,1024]{2,1,0:T(8,128)(2,1)}) %all-gather.7.cloned.1.call-update) | async-done | bytes 8388624 | tf_op jit(solution)/shard_map/all_gather | solution.py:42
  238.4 120.9 %while.20 = (s32[]{:T(128)}, bf16[128,1024]{1,0:T(8,128)(2,1)S(1)}, f32[128,1024]{1,0:T(8,128)S(1)}, bf16[1024,2112]{1,0:T(8,128)(2,1)}, bf16[1024,2112]{1,0:T(8,128)(2,1)}, /*index=5*/s32[]{:T(128)}) while((s32[]{:T(128)}, bf16[128,1024]{1,0:T(8,128)(2,1)S(1)}, f32[128,1024]{1,0:T(8,128)S(1)}, bf16[1024,2112]{1,0:T(8,128)(2,1)}, ...), condition=%wide.region_2.3_spmd, body=%wide.region_0.0_spmd.sunk | while | flops 1110220928 | bytes 11536493 | solution.py:69
  365.7 133.4 %while.21 = (s32[]{:T(128)}, bf16[128,1024]{1,0:T(8,128)(2,1)S(1)}, f32[128,1024]{1,0:T(8,128)S(1)}, f32[128,1]{0,1:T(1,128)S(1)}, bf16[1024,2112]{1,0:T(8,128)(...) while((s32[]{:T(128)}, bf16[128,1024]{1,0:T(8,128)(2,1)S(1)}, ...), condition=%wide.region_6.7_spmd, body=%wide.region_4.6_spmd.sunk | while | flops 1109409792 | bytes 14715525 | solution.py:91
  365.7 8.2 %multiply_reduce_fusion.7 = (f32[128]{0:T(128)S(1)}, f32[128,1024]{1,0:T(8,128)S(1)}) fusion(f32[128,1024]{1,0:T(8,128)S(1)} %get-tuple-element.292, bf16[1024,2112]{1,0:T(8,128)(2,1)} %get-tuple-element.291, f32[128,2112]{0,1:T(8,128)S(1)} %get-tuple-element.290, bf16[1024,2112]{1,0:T(8,128)(2,1)} %get-tuple-element.289, ...), kind=kOutput, calls=%fused_computation.16.clone.1 | convolution fusion | flops 1108492160 | bytes 11567616 | tf_op jit(solution)/shard_map/while/body/eval_jaxpr/dot_general | solution.py:26
  375.5 9.5 %collective-permute-done.1 = bf16[128,1024]{1,0:T(8,128)(2,1)S(1)} collective-permute-done((bf16[128,1024]{1,0:T(8,128)(2,1)S(1)}, bf16[128,1024]{1,0:T(8,128)(2,1)S(1)}, u32[]{:S(2)}, u32[]{:S(2)}) %collective-permute-start.1) | collective-permute-done | bytes 262176 | tf_op jit(solution)/shard_map/while/body/eval_jaxpr/ppermute | solution.py:12
  385.0 8.2 %multiply_reduce_fusion.7 = (f32[128]{0:T(128)S(1)}, f32[128,1024]{1,0:T(8,128)S(1)}) fusion(f32[128,1024]{1,0:T(8,128)S(1)} %get-tuple-element.292, bf16[1024,2112]{1,0:T(8,128)(2,1)} %get-tuple-element.291, f32[128,2112]{0,1:T(8,128)S(1)} %get-tuple-element.290, bf16[1024,2112]{1,0:T(8,128)(2,1)} %get-tuple-element.289, ...), kind=kOutput, calls=%fused_computation.16.clone.1 | convolution fusion | flops 1108492160 | bytes 11567616 | tf_op jit(solution)/shard_map/while/body/eval_jaxpr/dot_general | solution.py:26
  394.7 9.5 %collective-permute-done.1 = bf16[128,1024]{1,0:T(8,128)(2,1)S(1)} collective-permute-done((bf16[128,1024]{1,0:T(8,128)(2,1)S(1)}, bf16[128,1024]{1,0:T(8,128)(2,1)S(1)}, u32[]{:S(2)}, u32[]{:S(2)}) %collective-permute-start.1) | collective-permute-done | bytes 262176 | tf_op jit(solution)/shard_map/while/body/eval_jaxpr/ppermute | solution.py:12
  404.3 8.2 %multiply_reduce_fusion.7 = (f32[128]{0:T(128)S(1)}, f32[128,1024]{1,0:T(8,128)S(1)}) fusion(f32[128,1024]{1,0:T(8,128)S(1)} %get-tuple-element.292, bf16[1024,2112]{1,0:T(8,128)(2,1)} %get-tuple-element.291, f32[128,2112]{0,1:T(8,128)S(1)} %get-tuple-element.290, bf16[1024,2112]{1,0:T(8,128)(2,1)} %get-tuple-element.289, ...), kind=kOutput, calls=%fused_computation.16.clone.1 | convolution fusion | flops 1108492160 | bytes 11567616 | tf_op jit(solution)/shard_map/while/body/eval_jaxpr/dot_general | solution.py:26
  414.0 9.5 %collective-permute-done.1 = bf16[128,1024]{1,0:T(8,128)(2,1)S(1)} collective-permute-done((bf16[128,1024]{1,0:T(8,128)(2,1)S(1)}, bf16[128,1024]{1,0:T(8,128)(2,1)S(1)}, u32[]{:S(2)}, u32[]{:S(2)}) %collective-permute-start.1) | collective-permute-done | bytes 262176 | tf_op jit(solution)/shard_map/while/body/eval_jaxpr/ppermute | solution.py:12
  423.5 8.2 %multiply_reduce_fusion.7 = (f32[128]{0:T(128)S(1)}, f32[128,1024]{1,0:T(8,128)S(1)}) fusion(f32[128,1024]{1,0:T(8,128)S(1)} %get-tuple-element.292, bf16[1024,2112]{1,0:T(8,128)(2,1)} %get-tuple-element.291, f32[128,2112]{0,1:T(8,128)S(1)} %get-tuple-element.290, bf16[1024,2112]{1,0:T(8,128)(2,1)} %get-tuple-element.289, ...), kind=kOutput, calls=%fused_computation.16.clone.1 | convolution fusion | flops 1108492160 | bytes 11567616 | tf_op jit(solution)/shard_map/while/body/eval_jaxpr/dot_general | solution.py:26
  433.2 9.5 %collective-permute-done.1 = bf16[128,1024]{1,0:T(8,128)(2,1)S(1)} collective-permute-done((bf16[128,1024]{1,0:T(8,128)(2,1)S(1)}, bf16[128,1024]{1,0:T(8,128)(2,1)S(1)}, u32[]{:S(2)}, u32[]{:S(2)}) %collective-permute-start.1) | collective-permute-done | bytes 262176 | tf_op jit(solution)/shard_map/while/body/eval_jaxpr/ppermute | solution.py:12
  452.5 9.1 %collective-permute-done.1 = bf16[128,1024]{1,0:T(8,128)(2,1)S(1)} collective-permute-done((bf16[128,1024]{1,0:T(8,128)(2,1)S(1)}, bf16[128,1024]{1,0:T(8,128)(2,1)S(1)}, u32[]{:S(2)}, u32[]{:S(2)}) %collective-permute-start.1) | collective-permute-done | bytes 262176 | tf_op jit(solution)/shard_map/while/body/eval_jaxpr/ppermute | solution.py:12
  461.6 8.2 %multiply_reduce_fusion.7 = (f32[128]{0:T(128)S(1)}, f32[128,1024]{1,0:T(8,128)S(1)}) fusion(f32[128,1024]{1,0:T(8,128)S(1)} %get-tuple-element.292, bf16[1024,2112]{1,0:T(8,128)(2,1)} %get-tuple-element.291, f32[128,2112]{0,1:T(8,128)S(1)} %get-tuple-element.290, bf16[1024,2112]{1,0:T(8,128)(2,1)} %get-tuple-element.289, ...), kind=kOutput, calls=%fused_computation.16.clone.1 | convolution fusion | flops 1108492160 | bytes 11567616 | tf_op jit(solution)/shard_map/while/body/eval_jaxpr/dot_general | solution.py:26
  471.3 9.1 %collective-permute-done.1 = bf16[128,1024]{1,0:T(8,128)(2,1)S(1)} collective-permute-done((bf16[128,1024]{1,0:T(8,128)(2,1)S(1)}, bf16[128,1024]{1,0:T(8,128)(2,1)S(1)}, u32[]{:S(2)}, u32[]{:S(2)}) %collective-permute-start.1) | collective-permute-done | bytes 262176 | tf_op jit(solution)/shard_map/while/body/eval_jaxpr/ppermute | solution.py:12
  480.4 8.2 %multiply_reduce_fusion.7 = (f32[128]{0:T(128)S(1)}, f32[128,1024]{1,0:T(8,128)S(1)}) fusion(f32[128,1024]{1,0:T(8,128)S(1)} %get-tuple-element.292, bf16[1024,2112]{1,0:T(8,128)(2,1)} %get-tuple-element.291, f32[128,2112]{0,1:T(8,128)S(1)} %get-tuple-element.290, bf16[1024,2112]{1,0:T(8,128)(2,1)} %get-tuple-element.289, ...), kind=kOutput, calls=%fused_computation.16.clone.1 | convolution fusion | flops 1108492160 | bytes 11567616 | tf_op jit(solution)/shard_map/while/body/eval_jaxpr/dot_general | solution.py:26
  490.1 9.1 %collective-permute-done.1 = bf16[128,1024]{1,0:T(8,128)(2,1)S(1)} collective-permute-done((bf16[128,1024]{1,0:T(8,128)(2,1)S(1)}, bf16[128,1024]{1,0:T(8,128)(2,1)S(1)}, u32[]{:S(2)}, u32[]{:S(2)}) %collective-permute-start.1) | collective-permute-done | bytes 262176 | tf_op jit(solution)/shard_map/while/body/eval_jaxpr/ppermute | solution.py:12
  532.8 118.3 %fusion.49 = (bf16[1024,136]{0,1:T(8,128)(2,1)S(1)}, bf16[1024,136]{0,1:T(8,128)(2,1)S(1)}) fusion(bf16[1024,2112]{0,1:T(8,128)(2,1)} %convolution_convert_fusion.1, bf16[1024,2112]{0,1:T(8,128)(2,1)} %convolution_convert_fusion), kind=kCustom, calls=%all-reduce-scatter.2 | all-reduce-scatter fusion | flops 4456449 | bytes 9208320
  651.1 10.0 %collective-permute-start.3 = (bf16[1024,60]{0,1:T(8,128)(2,1)S(1)}, bf16[1024,60]{0,1:T(8,128)(2,1)S(1)}, u32[]{:S(2)}, u32[]{:S(2)}) collective-permute-start(bf16[1024,60]{0,1:T(8,128)(2,1)S(1)} %slice.3), channel_id=1, source_target_pairs={{0,8},{8,16},{16,24},{24,32},{32,40},{40,48},{48,56},{56,64},{64,7... | collective-permute-start | bytes 368648
  674.2 31.9 %reduce-scatter.8.cloned.1.call-done = bf16[128,512]{1,0:T(8,128)(2,1)} async-done(((bf16[128,4096]{1,0:T(8,128)(2,1)}), bf16[128,512]{1,0:T(8,128)(2,1)}) %reduce-scatter.8.cloned.1.call-update) | async-done | bytes 131088 | tf_op jit(solution)/shard_map/reduce_scatter | solution.py:107
  706.1 73.9 %reduce-scatter.12.cloned.1.call-done = bf16[64,1024]{1,0:T(8,128)(2,1)} async-done(((bf16[1024,1024]{1,0:T(8,128)(2,1)}), bf16[64,1024]{1,0:T(8,128)(2,1)}) %reduce-scatter.12.cloned.1.call-update) | async-done | bytes 131088 | tf_op jit(solution)/shard_map/reduce_scatter | solution.py:122
  (121 shorter events, 204.0 us)
Async XLA Ops:
  7.2 79.5 %all-gather.9.cloned.1.call-start = ((), (), s32[]{:S(2)}) async-start(), calls=%async_computation.7 | async-start | bytes 9191424 | tf_op jit(solution)/shard_map/all_gather | solution.py:51
  9.6 151.1 %all-gather.11.cloned.1.call-start = ((), (), s32[]{:S(2)}) async-start(), calls=%async_computation.8 | async-start | bytes 9191424 | tf_op jit(solution)/shard_map/all_gather | solution.py:52
  11.9 221.9 %all-gather.7.cloned.1.call-start = ((), (), s32[]{:S(2)}) async-start(), calls=%async_computation.6 | async-start | bytes 8912896 | tf_op jit(solution)/shard_map/all_gather | solution.py:42
  12.6 659.5 %reduce-scatter.10.cloned.1.call-start = ((), (), s32[]{:S(2)}) async-start(), calls=%async_computation.4 | async-start | bytes 8912896 | tf_op jit(solution)/shard_map/reduce_scatter | solution.py:116
  246.8 9.4 %collective-permute-start = (bf16[128,1024]{1,0:T(8,128)(2,1)S(1)}, bf16[128,1024]{1,0:T(8,128)(2,1)S(1)}, u32[]{:S(2)}, u32[]{:S(2)}) collective-permute-start(bf16[128,1024]{1,0:T(8,128)(2,1)S(1)} %fusion.71), channel_id=1, source_target_pairs={{0,1},{1,2},{2,3},{3,4},{4,5},{5,6},{6,7},{8,9},{9,10},{10,11},{11... | collective-permute-start | bytes 786440 | tf_op jit(solution)/shard_map/while/body/eval_jaxpr/ppermute | solution.py:12
  264.5 9.5 %collective-permute-start = (bf16[128,1024]{1,0:T(8,128)(2,1)S(1)}, bf16[128,1024]{1,0:T(8,128)(2,1)S(1)}, u32[]{:S(2)}, u32[]{:S(2)}) collective-permute-start(bf16[128,1024]{1,0:T(8,128)(2,1)S(1)} %fusion.71), channel_id=1, source_target_pairs={{0,1},{1,2},{2,3},{3,4},{4,5},{5,6},{6,7},{8,9},{9,10},{10,11},{11... | collective-permute-start | bytes 786440 | tf_op jit(solution)/shard_map/while/body/eval_jaxpr/ppermute | solution.py:12
  282.4 8.6 %collective-permute-start = (bf16[128,1024]{1,0:T(8,128)(2,1)S(1)}, bf16[128,1024]{1,0:T(8,128)(2,1)S(1)}, u32[]{:S(2)}, u32[]{:S(2)}) collective-permute-start(bf16[128,1024]{1,0:T(8,128)(2,1)S(1)} %fusion.71), channel_id=1, source_target_pairs={{0,1},{1,2},{2,3},{3,4},{4,5},{5,6},{6,7},{8,9},{9,10},{10,11},{11... | collective-permute-start | bytes 786440 | tf_op jit(solution)/shard_map/while/body/eval_jaxpr/ppermute | solution.py:12
  299.3 8.3 %collective-permute-start = (bf16[128,1024]{1,0:T(8,128)(2,1)S(1)}, bf16[128,1024]{1,0:T(8,128)(2,1)S(1)}, u32[]{:S(2)}, u32[]{:S(2)}) collective-permute-start(bf16[128,1024]{1,0:T(8,128)(2,1)S(1)} %fusion.71), channel_id=1, source_target_pairs={{0,1},{1,2},{2,3},{3,4},{4,5},{5,6},{6,7},{8,9},{9,10},{10,11},{11... | collective-permute-start | bytes 786440 | tf_op jit(solution)/shard_map/while/body/eval_jaxpr/ppermute | solution.py:12
  315.9 8.3 %collective-permute-start = (bf16[128,1024]{1,0:T(8,128)(2,1)S(1)}, bf16[128,1024]{1,0:T(8,128)(2,1)S(1)}, u32[]{:S(2)}, u32[]{:S(2)}) collective-permute-start(bf16[128,1024]{1,0:T(8,128)(2,1)S(1)} %fusion.71), channel_id=1, source_target_pairs={{0,1},{1,2},{2,3},{3,4},{4,5},{5,6},{6,7},{8,9},{9,10},{10,11},{11... | collective-permute-start | bytes 786440 | tf_op jit(solution)/shard_map/while/body/eval_jaxpr/ppermute | solution.py:12
  332.5 8.3 %collective-permute-start = (bf16[128,1024]{1,0:T(8,128)(2,1)S(1)}, bf16[128,1024]{1,0:T(8,128)(2,1)S(1)}, u32[]{:S(2)}, u32[]{:S(2)}) collective-permute-start(bf16[128,1024]{1,0:T(8,128)(2,1)S(1)} %fusion.71), channel_id=1, source_target_pairs={{0,1},{1,2},{2,3},{3,4},{4,5},{5,6},{6,7},{8,9},{9,10},{10,11},{11... | collective-permute-start | bytes 786440 | tf_op jit(solution)/shard_map/while/body/eval_jaxpr/ppermute | solution.py:12
  349.1 10.3 %collective-permute-start = (bf16[128,1024]{1,0:T(8,128)(2,1)S(1)}, bf16[128,1024]{1,0:T(8,128)(2,1)S(1)}, u32[]{:S(2)}, u32[]{:S(2)}) collective-permute-start(bf16[128,1024]{1,0:T(8,128)(2,1)S(1)} %fusion.71), channel_id=1, source_target_pairs={{0,1},{1,2},{2,3},{3,4},{4,5},{5,6},{6,7},{8,9},{9,10},{10,11},{11... | collective-permute-start | bytes 786440 | tf_op jit(solution)/shard_map/while/body/eval_jaxpr/ppermute | solution.py:12
  374.2 10.8 %collective-permute-start.1 = (bf16[128,1024]{1,0:T(8,128)(2,1)S(1)}, bf16[128,1024]{1,0:T(8,128)(2,1)S(1)}, u32[]{:S(2)}, u32[]{:S(2)}) collective-permute-start(bf16[128,1024]{1,0:T(8,128)(2,1)S(1)} %add_convert_fusion.3), channel_id=1, source_target_pairs={{1,0},{2,1},{3,2},{4,3},{5,4},{6,5},{7,6},{9,8},{10,9},{11,10},{12... | collective-permute-start | bytes 786440 | tf_op jit(solution)/shard_map/while/body/eval_jaxpr/ppermute | solution.py:12
  393.4 10.8 %collective-permute-start.1 = (bf16[128,1024]{1,0:T(8,128)(2,1)S(1)}, bf16[128,1024]{1,0:T(8,128)(2,1)S(1)}, u32[]{:S(2)}, u32[]{:S(2)}) collective-permute-start(bf16[128,1024]{1,0:T(8,128)(2,1)S(1)} %add_convert_fusion.3), channel_id=1, source_target_pairs={{1,0},{2,1},{3,2},{4,3},{5,4},{6,5},{7,6},{9,8},{10,9},{11,10},{12... | collective-permute-start | bytes 786440 | tf_op jit(solution)/shard_map/while/body/eval_jaxpr/ppermute | solution.py:12
  412.7 10.8 %collective-permute-start.1 = (bf16[128,1024]{1,0:T(8,128)(2,1)S(1)}, bf16[128,1024]{1,0:T(8,128)(2,1)S(1)}, u32[]{:S(2)}, u32[]{:S(2)}) collective-permute-start(bf16[128,1024]{1,0:T(8,128)(2,1)S(1)} %add_convert_fusion.3), channel_id=1, source_target_pairs={{1,0},{2,1},{3,2},{4,3},{5,4},{6,5},{7,6},{9,8},{10,9},{11,10},{12... | collective-permute-start | bytes 786440 | tf_op jit(solution)/shard_map/while/body/eval_jaxpr/ppermute | solution.py:12
  431.9 10.8 %collective-permute-start.1 = (bf16[128,1024]{1,0:T(8,128)(2,1)S(1)}, bf16[128,1024]{1,0:T(8,128)(2,1)S(1)}, u32[]{:S(2)}, u32[]{:S(2)}) collective-permute-start(bf16[128,1024]{1,0:T(8,128)(2,1)S(1)} %add_convert_fusion.3), channel_id=1, source_target_pairs={{1,0},{2,1},{3,2},{4,3},{5,4},{6,5},{7,6},{9,8},{10,9},{11,10},{12... | collective-permute-start | bytes 786440 | tf_op jit(solution)/shard_map/while/body/eval_jaxpr/ppermute | solution.py:12
  451.2 10.4 %collective-permute-start.1 = (bf16[128,1024]{1,0:T(8,128)(2,1)S(1)}, bf16[128,1024]{1,0:T(8,128)(2,1)S(1)}, u32[]{:S(2)}, u32[]{:S(2)}) collective-permute-start(bf16[128,1024]{1,0:T(8,128)(2,1)S(1)} %add_convert_fusion.3), channel_id=1, source_target_pairs={{1,0},{2,1},{3,2},{4,3},{5,4},{6,5},{7,6},{9,8},{10,9},{11,10},{12... | collective-permute-start | bytes 786440 | tf_op jit(solution)/shard_map/while/body/eval_jaxpr/ppermute | solution.py:12
  470.0 10.4 %collective-permute-start.1 = (bf16[128,1024]{1,0:T(8,128)(2,1)S(1)}, bf16[128,1024]{1,0:T(8,128)(2,1)S(1)}, u32[]{:S(2)}, u32[]{:S(2)}) collective-permute-start(bf16[128,1024]{1,0:T(8,128)(2,1)S(1)} %add_convert_fusion.3), channel_id=1, source_target_pairs={{1,0},{2,1},{3,2},{4,3},{5,4},{6,5},{7,6},{9,8},{10,9},{11,10},{12... | collective-permute-start | bytes 786440 | tf_op jit(solution)/shard_map/while/body/eval_jaxpr/ppermute | solution.py:12
  488.8 10.4 %collective-permute-start.1 = (bf16[128,1024]{1,0:T(8,128)(2,1)S(1)}, bf16[128,1024]{1,0:T(8,128)(2,1)S(1)}, u32[]{:S(2)}, u32[]{:S(2)}) collective-permute-start(bf16[128,1024]{1,0:T(8,128)(2,1)S(1)} %add_convert_fusion.3), channel_id=1, source_target_pairs={{1,0},{2,1},{3,2},{4,3},{5,4},{6,5},{7,6},{9,8},{10,9},{11,10},{12... | collective-permute-start | bytes 786440 | tf_op jit(solution)/shard_map/while/body/eval_jaxpr/ppermute | solution.py:12
  515.8 190.3 %reduce-scatter.8.cloned.1.call-start = ((), (), s32[]{:S(2)}) async-start(), calls=%async_computation.3 | async-start | bytes 1179648 | tf_op jit(solution)/shard_map/reduce_scatter | solution.py:107
  523.1 256.8 %reduce-scatter.12.cloned.1.call-start = ((), (), s32[]{:S(2)}) async-start(), calls=%async_computation.5 | async-start | bytes 2228224 | tf_op jit(solution)/shard_map/reduce_scatter | solution.py:122
  532.7 134.9 %copy-start.6 = (u32[128]{0:T(128)S(1)}, u32[128]{0:T(128)}, u32[]{:S(2)}) copy-start(u32[128]{0:T(128)} %constant.72) | copy-start | bytes 1540
  532.7 247.2 %copy-start.1 = (bf16[1,1024,1024]{2,1,0:T(8,128)(2,1)S(1)}, bf16[1,1024,1024]{2,1,0:T(8,128)(2,1)}, u32[]{:S(2)}) copy-start(bf16[1,1024,1024]{2,1,0:T(8,128)(2,1)} %param.14) | copy-start | bytes 6291460
  651.1 17.9 %collective-permute-start.3 = (bf16[1024,60]{0,1:T(8,128)(2,1)S(1)}, bf16[1024,60]{0,1:T(8,128)(2,1)S(1)}, u32[]{:S(2)}, u32[]{:S(2)}) collective-permute-start(bf16[1024,60]{0,1:T(8,128)(2,1)S(1)} %slice.3), channel_id=1, source_target_pairs={{0,8},{8,16},{16,24},{24,32},{32,40},{40,48},{48,56},{56,64},{64,7... | collective-permute-start | bytes 368648
  661.1 8.1 %collective-permute-start.2 = (bf16[1024,60]{0,1:T(8,128)(2,1)S(1)}, bf16[1024,60]{0,1:T(8,128)(2,1)}, u32[]{:S(2)}, u32[]{:S(2)}) collective-permute-start(bf16[1024,60]{0,1:T(8,128)(2,1)S(1)} %slice.2), channel_id=1, source_target_pairs={{0,8},{8,16},{16,24},{24,32},{32,40},{40,48},{48,56},{56,64},{64,7... | collective-permute-start | bytes 368648
  (6 other events, 283.0 us)
Sparse Core Ops, SparseCore 0:
  10.4 76.2 all-gather.8
  89.1 71.6 all-gather.10
  163.2 70.5 all-gather.6
  515.9 148.7 reduce-scatter.9
  667.5 38.5 reduce-scatter.7
  710.4 69.4 reduce-scatter.11
where the time goes:
time: 789 us; the launch traced here: 787 us
  waiting for transfers between devices  380 us (48%)
  matrix products  158 us (20%)
  blocking collectives  118 us (15%)
  starting transfers between devices  57.7 us (7%)
  local copies, waits for them, and re-layouts  53.7 us (7%)
  between operations  15 us (2%)
    dot_general x16, matrix products, contract_cols(): lax.dot_general(left, right, (((1,), (1,)), ((), ())), preferred_element_...  127 us
    unnamed x1, blocking collectives  118 us
    ppermute x14, waiting for transfers between devices, shifted(): return lax.ppermute(block, axis, route)  96.1 us
    reduce_scatter x1, waiting for transfers between devices, per_device(): lax.psum_scatter(contract_rows(onehot, carried).astype(jnp.bfloat16), 'dp...  73.9 us
    all_gather x1, waiting for transfers between devices, per_device(): lax.all_gather(depth_w1[0], 'dp', axis=1, tiled=True)  71.7 us
    all_gather x1, waiting for transfers between devices, per_device(): lax.all_gather(depth_w2[0], 'dp', axis=1, tiled=True)  53.2 us
    all_gather x1, waiting for transfers between devices, per_device(): projection = lax.all_gather(depth_in[0], 'dp', axis=0, tiled=True)  52.1 us
    unnamed x26, local copies, waits for them, and re-layouts  50.6 us
  transfers between devices with their start and end apart: 22, of which 19 were waited for; matrix products, arithmetic and copies ran while one was open for 24% of the time, Pallas kernels for 0%

commit v1 on v0

--- a/solution.py
+++ b/solution.py
@@ -48,7 +48,9 @@
     )
     width_depth = depth_base.shape[1]
     w_first, w_second = (
-        lax.all_gather(depth_w1[0], "dp", axis=1, tiled=True),
+        jnp.concatenate(
+            lax.all_to_all(jnp.stack([depth_w1[0]] * lax.axis_size("dp")), "dp", 0, 0), axis=1
+        ),
         lax.all_gather(depth_w2[0], "dp", axis=1, tiled=True),
     )
 

time: 789 us -> 754 us (0.956)
  waiting for transfers between devices: 380 us -> 349 us
    all_to_all x0 -> x1, waiting for transfers between devices: none -> 73.9 us  [per_device(): lax.all_to_all(jnp.stack([depth_w1[0]] * lax.axis_size('dp')), 'dp', 0, 0)]
    all_gather x1 -> x0, waiting for transfers between devices: 71.7 us -> none  [per_device(): lax.all_gather(depth_w1[0], 'dp', axis=1, tiled=True)]
    all_gather x1, waiting for transfers between devices: 53.2 us -> 13.7 us  [per_device(): lax.all_gather(depth_w2[0], 'dp', axis=1, tiled=True)]
    unnamed x26, local copies, waits for them, and re-layouts: 50.6 us -> 27.5 us
where the time goes in v1:
time: 754 us; the launch traced here: 753 us
  waiting for transfers between devices  349 us (46%)
  matrix products  154 us (20%)
  blocking collectives  118 us (16%)
  starting transfers between devices  65.1 us (9%)
  local copies, waits for them, and re-layouts  47.6 us (6%)
  between operations  14.6 us (2%)
    dot_general x16, matrix products, contract_cols(): lax.dot_general(left, right, (((1,), (1,)), ((), ())), preferred_element_...  125 us
    unnamed x1, blocking collectives  118 us
    ppermute x14, waiting for transfers between devices, shifted(): return lax.ppermute(block, axis, route)  96.1 us
    all_to_all x1, waiting for transfers between devices, per_device(): lax.all_to_all(jnp.stack([depth_w1[0]] * lax.axis_size('dp')), 'dp', 0, 0)  73.9 us
    reduce_scatter x1, waiting for transfers between devices, per_device(): lax.psum_scatter(contract_rows(onehot, carried).astype(jnp.bfloat16), 'dp...  73.8 us
    all_gather x1, waiting for transfers between devices, per_device(): projection = lax.all_gather(depth_in[0], 'dp', axis=0, tiled=True)  58.9 us
    ppermute x14, starting transfers between devices, shifted(): return lax.ppermute(block, axis, route)  40.9 us
    reduce_scatter x1, waiting for transfers between devices, per_device(): lax.psum_scatter(contract_cols(carried, projection).astype(jnp.bfloat16),...  31.9 us
  transfers between devices with their start and end apart: 22, of which 19 were waited for; matrix products, arithmetic and copies ran while one was open for 24% of the time, Pallas kernels for 0%

profile of v1, /device:TPU:0, one launch (start us, length us, event | category | flops | bytes accessed | tf_op | source)
XLA Modules:
  0.0 752.7 jit_solution(6084625210522888029)
XLA Ops:
  23.0 73.9 %all-to-all-done = bf16[16,1024,132]{1,2,0:T(8,128)(2,1)} async-done(((bf16[16,1024,132]{1,2,0:T(8,128)(2,1)}), bf16[16,1024,132]{1,2,0:T(8,128)(2,1)}, u32[]{:S(2)}, u32[]{:S(2)}) %all-to-all-start) | async-done | bytes 4325408 | tf_op jit(solution)/shard_map/all_to_all | solution.py:52
  110.3 13.7 %all-gather.7.cloned.1.call-done = bf16[1,1024,2112]{1,0,2:T(2,128)(2,1)} async-done(((bf16[1,1024,132]{1,0,2:T(2,128)(2,1)}), bf16[1,1024,2112]{1,0,2:T(2,128)(2,1)}) %all-gather.7.cloned.1.call-update) | async-done | bytes 4325392 | tf_op jit(solution)/shard_map/all_gather | solution.py:54
  123.9 20.8 %copy.35 = bf16[1,1024,2112]{2,1,0:T(8,128)(2,1)} copy(bf16[1,1024,2112]{1,0,2:T(2,128)(2,1)} %all-gather.7.cloned.1.call-done) | data formatting | bytes 8650752
  144.8 58.9 %all-gather.5.cloned.1.call-done = bf16[1,4096,1024]{2,1,0:T(8,128)(2,1)} async-done(((bf16[1,256,1024]{2,1,0:T(8,128)(2,1)}), bf16[1,4096,1024]{2,1,0:T(8,128)(2,1)}) %all-gather.5.cloned.1.call-update) | async-done | bytes 8388624 | tf_op jit(solution)/shard_map/all_gather | solution.py:42
  208.3 120.9 %while.20 = (s32[]{:T(128)}, bf16[128,1024]{1,0:T(8,128)(2,1)S(1)}, f32[128,1024]{1,0:T(8,128)S(1)}, bf16[1024,2112]{1,0:T(8,128)(2,1)}, bf16[1024,2112]{1,0:T(8,128)(2,1)}, /*index=5*/s32[]{:T(128)}) while((s32[]{:T(128)}, bf16[128,1024]{1,0:T(8,128)(2,1)S(1)}, f32[128,1024]{1,0:T(8,128)S(1)}, bf16[1024,2112]{1,0:T(8,128)(2,1)}, ...), condition=%wide.region_2.3_spmd, body=%wide.region_0.0_spmd.sunk | while | flops 1110220928 | bytes 11536493 | solution.py:71
  334.1 133.4 %while.21 = (s32[]{:T(128)}, bf16[128,1024]{1,0:T(8,128)(2,1)S(1)}, f32[128,1024]{1,0:T(8,128)S(1)}, f32[128,1]{0,1:T(1,128)S(1)}, bf16[1024,2112]{1,0:T(8,128)(...) while((s32[]{:T(128)}, bf16[128,1024]{1,0:T(8,128)(2,1)S(1)}, ...), condition=%wide.region_6.7_spmd, body=%wide.region_4.6_spmd.sunk | while | flops 1109409792 | bytes 14715525 | solution.py:93
  334.1 8.2 %multiply_reduce_fusion.7 = (f32[128]{0:T(128)S(1)}, f32[128,1024]{1,0:T(8,128)S(1)}) fusion(f32[128,1024]{1,0:T(8,128)S(1)} %get-tuple-element.310, bf16[1024,2112]{1,0:T(8,128)(2,1)} %get-tuple-element.309, f32[128,2112]{0,1:T(8,128)S(1)} %get-tuple-element.308, bf16[1024,2112]{1,0:T(8,128)(2,1)} %get-tuple-element.307, ...), kind=kOutput, calls=%fused_computation.16.clone.1 | convolution fusion | flops 1108492160 | bytes 11567616 | tf_op jit(solution)/shard_map/while/body/eval_jaxpr/dot_general | solution.py:26
  343.8 9.5 %collective-permute-done.1 = bf16[128,1024]{1,0:T(8,128)(2,1)S(1)} collective-permute-done((bf16[128,1024]{1,0:T(8,128)(2,1)S(1)}, bf16[128,1024]{1,0:T(8,128)(2,1)S(1)}, u32[]{:S(2)}, u32[]{:S(2)}) %collective-permute-start.1) | collective-permute-done | bytes 262176 | tf_op jit(solution)/shard_map/while/body/eval_jaxpr/ppermute | solution.py:12
  353.4 8.2 %multiply_reduce_fusion.7 = (f32[128]{0:T(128)S(1)}, f32[128,1024]{1,0:T(8,128)S(1)}) fusion(f32[128,1024]{1,0:T(8,128)S(1)} %get-tuple-element.310, bf16[1024,2112]{1,0:T(8,128)(2,1)} %get-tuple-element.309, f32[128,2112]{0,1:T(8,128)S(1)} %get-tuple-element.308, bf16[1024,2112]{1,0:T(8,128)(2,1)} %get-tuple-element.307, ...), kind=kOutput, calls=%fused_computation.16.clone.1 | convolution fusion | flops 1108492160 | bytes 11567616 | tf_op jit(solution)/shard_map/while/body/eval_jaxpr/dot_general | solution.py:26
  363.1 9.5 %collective-permute-done.1 = bf16[128,1024]{1,0:T(8,128)(2,1)S(1)} collective-permute-done((bf16[128,1024]{1,0:T(8,128)(2,1)S(1)}, bf16[128,1024]{1,0:T(8,128)(2,1)S(1)}, u32[]{:S(2)}, u32[]{:S(2)}) %collective-permute-start.1) | collective-permute-done | bytes 262176 | tf_op jit(solution)/shard_map/while/body/eval_jaxpr/ppermute | solution.py:12
  372.6 8.2 %multiply_reduce_fusion.7 = (f32[128]{0:T(128)S(1)}, f32[128,1024]{1,0:T(8,128)S(1)}) fusion(f32[128,1024]{1,0:T(8,128)S(1)} %get-tuple-element.310, bf16[1024,2112]{1,0:T(8,128)(2,1)} %get-tuple-element.309, f32[128,2112]{0,1:T(8,128)S(1)} %get-tuple-element.308, bf16[1024,2112]{1,0:T(8,128)(2,1)} %get-tuple-element.307, ...), kind=kOutput, calls=%fused_computation.16.clone.1 | convolution fusion | flops 1108492160 | bytes 11567616 | tf_op jit(solution)/shard_map/while/body/eval_jaxpr/dot_general | solution.py:26
  382.3 9.5 %collective-permute-done.1 = bf16[128,1024]{1,0:T(8,128)(2,1)S(1)} collective-permute-done((bf16[128,1024]{1,0:T(8,128)(2,1)S(1)}, bf16[128,1024]{1,0:T(8,128)(2,1)S(1)}, u32[]{:S(2)}, u32[]{:S(2)}) %collective-permute-start.1) | collective-permute-done | bytes 262176 | tf_op jit(solution)/shard_map/while/body/eval_jaxpr/ppermute | solution.py:12
  391.9 8.2 %multiply_reduce_fusion.7 = (f32[128]{0:T(128)S(1)}, f32[128,1024]{1,0:T(8,128)S(1)}) fusion(f32[128,1024]{1,0:T(8,128)S(1)} %get-tuple-element.310, bf16[1024,2112]{1,0:T(8,128)(2,1)} %get-tuple-element.309, f32[128,2112]{0,1:T(8,128)S(1)} %get-tuple-element.308, bf16[1024,2112]{1,0:T(8,128)(2,1)} %get-tuple-element.307, ...), kind=kOutput, calls=%fused_computation.16.clone.1 | convolution fusion | flops 1108492160 | bytes 11567616 | tf_op jit(solution)/shard_map/while/body/eval_jaxpr/dot_general | solution.py:26
  401.6 9.5 %collective-permute-done.1 = bf16[128,1024]{1,0:T(8,128)(2,1)S(1)} collective-permute-done((bf16[128,1024]{1,0:T(8,128)(2,1)S(1)}, bf16[128,1024]{1,0:T(8,128)(2,1)S(1)}, u32[]{:S(2)}, u32[]{:S(2)}) %collective-permute-start.1) | collective-permute-done | bytes 262176 | tf_op jit(solution)/shard_map/while/body/eval_jaxpr/ppermute | solution.py:12
  411.1 8.2 %multiply_reduce_fusion.7 = (f32[128]{0:T(128)S(1)}, f32[128,1024]{1,0:T(8,128)S(1)}) fusion(f32[128,1024]{1,0:T(8,128)S(1)} %get-tuple-element.310, bf16[1024,2112]{1,0:T(8,128)(2,1)} %get-tuple-element.309, f32[128,2112]{0,1:T(8,128)S(1)} %get-tuple-element.308, bf16[1024,2112]{1,0:T(8,128)(2,1)} %get-tuple-element.307, ...), kind=kOutput, calls=%fused_computation.16.clone.1 | convolution fusion | flops 1108492160 | bytes 11567616 | tf_op jit(solution)/shard_map/while/body/eval_jaxpr/dot_general | solution.py:26
  420.8 9.1 %collective-permute-done.1 = bf16[128,1024]{1,0:T(8,128)(2,1)S(1)} collective-permute-done((bf16[128,1024]{1,0:T(8,128)(2,1)S(1)}, bf16[128,1024]{1,0:T(8,128)(2,1)S(1)}, u32[]{:S(2)}, u32[]{:S(2)}) %collective-permute-start.1) | collective-permute-done | bytes 262176 | tf_op jit(solution)/shard_map/while/body/eval_jaxpr/ppermute | solution.py:12
  429.9 8.2 %multiply_reduce_fusion.7 = (f32[128]{0:T(128)S(1)}, f32[128,1024]{1,0:T(8,128)S(1)}) fusion(f32[128,1024]{1,0:T(8,128)S(1)} %get-tuple-element.310, bf16[1024,2112]{1,0:T(8,128)(2,1)} %get-tuple-element.309, f32[128,2112]{0,1:T(8,128)S(1)} %get-tuple-element.308, bf16[1024,2112]{1,0:T(8,128)(2,1)} %get-tuple-element.307, ...), kind=kOutput, calls=%fused_computation.16.clone.1 | convolution fusion | flops 1108492160 | bytes 11567616 | tf_op jit(solution)/shard_map/while/body/eval_jaxpr/dot_general | solution.py:26
  439.6 9.1 %collective-permute-done.1 = bf16[128,1024]{1,0:T(8,128)(2,1)S(1)} collective-permute-done((bf16[128,1024]{1,0:T(8,128)(2,1)S(1)}, bf16[128,1024]{1,0:T(8,128)(2,1)S(1)}, u32[]{:S(2)}, u32[]{:S(2)}) %collective-permute-start.1) | collective-permute-done | bytes 262176 | tf_op jit(solution)/shard_map/while/body/eval_jaxpr/ppermute | solution.py:12
  448.7 8.2 %multiply_reduce_fusion.7 = (f32[128]{0:T(128)S(1)}, f32[128,1024]{1,0:T(8,128)S(1)}) fusion(f32[128,1024]{1,0:T(8,128)S(1)} %get-tuple-element.310, bf16[1024,2112]{1,0:T(8,128)(2,1)} %get-tuple-element.309, f32[128,2112]{0,1:T(8,128)S(1)} %get-tuple-element.308, bf16[1024,2112]{1,0:T(8,128)(2,1)} %get-tuple-element.307, ...), kind=kOutput, calls=%fused_computation.16.clone.1 | convolution fusion | flops 1108492160 | bytes 11567616 | tf_op jit(solution)/shard_map/while/body/eval_jaxpr/dot_general | solution.py:26
  458.4 9.1 %collective-permute-done.1 = bf16[128,1024]{1,0:T(8,128)(2,1)S(1)} collective-permute-done((bf16[128,1024]{1,0:T(8,128)(2,1)S(1)}, bf16[128,1024]{1,0:T(8,128)(2,1)S(1)}, u32[]{:S(2)}, u32[]{:S(2)}) %collective-permute-start.1) | collective-permute-done | bytes 262176 | tf_op jit(solution)/shard_map/while/body/eval_jaxpr/ppermute | solution.py:12
  499.0 118.2 %fusion.44 = (bf16[1024,136]{0,1:T(8,128)(2,1)S(1)}, bf16[1024,136]{0,1:T(8,128)(2,1)S(1)}) fusion(bf16[1024,2112]{0,1:T(8,128)(2,1)} %convolution_convert_fusion.1, bf16[1024,2112]{0,1:T(8,128)(2,1)} %convolution_convert_fusion), kind=kCustom, calls=%all-reduce-scatter.2 | all-reduce-scatter fusion | flops 4456449 | bytes 9208320
  617.3 10.1 %collective-permute-start.3 = (bf16[1024,60]{0,1:T(8,128)(2,1)S(1)}, bf16[1024,60]{0,1:T(8,128)(2,1)S(1)}, u32[]{:S(2)}, u32[]{:S(2)}) collective-permute-start(bf16[1024,60]{0,1:T(8,128)(2,1)S(1)} %slice.3), channel_id=1, source_target_pairs={{0,8},{8,16},{16,24},{24,32},{32,40},{40,48},{48,56},{56,64},{64,7... | collective-permute-start | bytes 368648
  640.5 31.9 %reduce-scatter.8.cloned.1.call-done = bf16[128,512]{1,0:T(8,128)(2,1)} async-done(((bf16[128,4096]{1,0:T(8,128)(2,1)}), bf16[128,512]{1,0:T(8,128)(2,1)}) %reduce-scatter.8.cloned.1.call-update) | async-done | bytes 131088 | tf_op jit(solution)/shard_map/reduce_scatter | solution.py:109
  672.4 73.8 %reduce-scatter.12.cloned.1.call-done = bf16[64,1024]{1,0:T(8,128)(2,1)} async-done(((bf16[1024,1024]{1,0:T(8,128)(2,1)}), bf16[64,1024]{1,0:T(8,128)(2,1)}) %reduce-scatter.12.cloned.1.call-update) | async-done | bytes 131088 | tf_op jit(solution)/shard_map/reduce_scatter | solution.py:124
  (123 shorter events, 213.6 us)
Async XLA Ops:
  7.2 116.7 %all-gather.7.cloned.1.call-start = ((), (), s32[]{:S(2)}) async-start(), calls=%async_computation.8 | async-start | bytes 9191424 | tf_op jit(solution)/shard_map/all_gather | solution.py:54
  9.6 194.1 %all-gather.5.cloned.1.call-start = ((), (), s32[]{:S(2)}) async-start(), calls=%async_computation.7 | async-start | bytes 8912896 | tf_op jit(solution)/shard_map/all_gather | solution.py:42
  13.9 82.9 %all-to-all-start = ((bf16[16,1024,132]{1,2,0:T(8,128)(2,1)}), bf16[16,1024,132]{1,2,0:T(8,128)(2,1)}, u32[]{:S(2)}, u32[]{:S(2)}) async-start(bf16[16,1024,132]{1,2,0:T(8,128)(2,1)} %stack.3), calls=%async_computation | async-start | bytes 8912896 | tf_op jit(solution)/shard_map/all_to_all | solution.py:52
  21.2 617.2 %reduce-scatter.10.cloned.1.call-start = ((), (), s32[]{:S(2)}) async-start(), calls=%async_computation.5 | async-start | bytes 8912896 | tf_op jit(solution)/shard_map/reduce_scatter | solution.py:118
  216.7 9.4 %collective-permute-start = (bf16[128,1024]{1,0:T(8,128)(2,1)S(1)}, bf16[128,1024]{1,0:T(8,128)(2,1)S(1)}, u32[]{:S(2)}, u32[]{:S(2)}) collective-permute-start(bf16[128,1024]{1,0:T(8,128)(2,1)S(1)} %fusion.68), channel_id=1, source_target_pairs={{0,1},{1,2},{2,3},{3,4},{4,5},{5,6},{6,7},{8,9},{9,10},{10,11},{11... | collective-permute-start | bytes 786440 | tf_op jit(solution)/shard_map/while/body/eval_jaxpr/ppermute | solution.py:12
  234.4 9.5 %collective-permute-start = (bf16[128,1024]{1,0:T(8,128)(2,1)S(1)}, bf16[128,1024]{1,0:T(8,128)(2,1)S(1)}, u32[]{:S(2)}, u32[]{:S(2)}) collective-permute-start(bf16[128,1024]{1,0:T(8,128)(2,1)S(1)} %fusion.68), channel_id=1, source_target_pairs={{0,1},{1,2},{2,3},{3,4},{4,5},{5,6},{6,7},{8,9},{9,10},{10,11},{11... | collective-permute-start | bytes 786440 | tf_op jit(solution)/shard_map/while/body/eval_jaxpr/ppermute | solution.py:12
  252.3 8.6 %collective-permute-start = (bf16[128,1024]{1,0:T(8,128)(2,1)S(1)}, bf16[128,1024]{1,0:T(8,128)(2,1)S(1)}, u32[]{:S(2)}, u32[]{:S(2)}) collective-permute-start(bf16[128,1024]{1,0:T(8,128)(2,1)S(1)} %fusion.68), channel_id=1, source_target_pairs={{0,1},{1,2},{2,3},{3,4},{4,5},{5,6},{6,7},{8,9},{9,10},{10,11},{11... | collective-permute-start | bytes 786440 | tf_op jit(solution)/shard_map/while/body/eval_jaxpr/ppermute | solution.py:12
  269.2 8.3 %collective-permute-start = (bf16[128,1024]{1,0:T(8,128)(2,1)S(1)}, bf16[128,1024]{1,0:T(8,128)(2,1)S(1)}, u32[]{:S(2)}, u32[]{:S(2)}) collective-permute-start(bf16[128,1024]{1,0:T(8,128)(2,1)S(1)} %fusion.68), channel_id=1, source_target_pairs={{0,1},{1,2},{2,3},{3,4},{4,5},{5,6},{6,7},{8,9},{9,10},{10,11},{11... | collective-permute-start | bytes 786440 | tf_op jit(solution)/shard_map/while/body/eval_jaxpr/ppermute | solution.py:12
  285.8 8.3 %collective-permute-start = (bf16[128,1024]{1,0:T(8,128)(2,1)S(1)}, bf16[128,1024]{1,0:T(8,128)(2,1)S(1)}, u32[]{:S(2)}, u32[]{:S(2)}) collective-permute-start(bf16[128,1024]{1,0:T(8,128)(2,1)S(1)} %fusion.68), channel_id=1, source_target_pairs={{0,1},{1,2},{2,3},{3,4},{4,5},{5,6},{6,7},{8,9},{9,10},{10,11},{11... | collective-permute-start | bytes 786440 | tf_op jit(solution)/shard_map/while/body/eval_jaxpr/ppermute | solution.py:12
  302.4 8.3 %collective-permute-start = (bf16[128,1024]{1,0:T(8,128)(2,1)S(1)}, bf16[128,1024]{1,0:T(8,128)(2,1)S(1)}, u32[]{:S(2)}, u32[]{:S(2)}) collective-permute-start(bf16[128,1024]{1,0:T(8,128)(2,1)S(1)} %fusion.68), channel_id=1, source_target_pairs={{0,1},{1,2},{2,3},{3,4},{4,5},{5,6},{6,7},{8,9},{9,10},{10,11},{11... | collective-permute-start | bytes 786440 | tf_op jit(solution)/shard_map/while/body/eval_jaxpr/ppermute | solution.py:12
  319.0 10.3 %collective-permute-start = (bf16[128,1024]{1,0:T(8,128)(2,1)S(1)}, bf16[128,1024]{1,0:T(8,128)(2,1)S(1)}, u32[]{:S(2)}, u32[]{:S(2)}) collective-permute-start(bf16[128,1024]{1,0:T(8,128)(2,1)S(1)} %fusion.68), channel_id=1, source_target_pairs={{0,1},{1,2},{2,3},{3,4},{4,5},{5,6},{6,7},{8,9},{9,10},{10,11},{11... | collective-permute-start | bytes 786440 | tf_op jit(solution)/shard_map/while/body/eval_jaxpr/ppermute | solution.py:12
  342.5 10.8 %collective-permute-start.1 = (bf16[128,1024]{1,0:T(8,128)(2,1)S(1)}, bf16[128,1024]{1,0:T(8,128)(2,1)S(1)}, u32[]{:S(2)}, u32[]{:S(2)}) collective-permute-start(bf16[128,1024]{1,0:T(8,128)(2,1)S(1)} %add_convert_fusion.3), channel_id=1, source_target_pairs={{1,0},{2,1},{3,2},{4,3},{5,4},{6,5},{7,6},{9,8},{10,9},{11,10},{12... | collective-permute-start | bytes 786440 | tf_op jit(solution)/shard_map/while/body/eval_jaxpr/ppermute | solution.py:12
  361.8 10.8 %collective-permute-start.1 = (bf16[128,1024]{1,0:T(8,128)(2,1)S(1)}, bf16[128,1024]{1,0:T(8,128)(2,1)S(1)}, u32[]{:S(2)}, u32[]{:S(2)}) collective-permute-start(bf16[128,1024]{1,0:T(8,128)(2,1)S(1)} %add_convert_fusion.3), channel_id=1, source_target_pairs={{1,0},{2,1},{3,2},{4,3},{5,4},{6,5},{7,6},{9,8},{10,9},{11,10},{12... | collective-permute-start | bytes 786440 | tf_op jit(solution)/shard_map/while/body/eval_jaxpr/ppermute | solution.py:12
  381.0 10.8 %collective-permute-start.1 = (bf16[128,1024]{1,0:T(8,128)(2,1)S(1)}, bf16[128,1024]{1,0:T(8,128)(2,1)S(1)}, u32[]{:S(2)}, u32[]{:S(2)}) collective-permute-start(bf16[128,1024]{1,0:T(8,128)(2,1)S(1)} %add_convert_fusion.3), channel_id=1, source_target_pairs={{1,0},{2,1},{3,2},{4,3},{5,4},{6,5},{7,6},{9,8},{10,9},{11,10},{12... | collective-permute-start | bytes 786440 | tf_op jit(solution)/shard_map/while/body/eval_jaxpr/ppermute | solution.py:12
  400.3 10.8 %collective-permute-start.1 = (bf16[128,1024]{1,0:T(8,128)(2,1)S(1)}, bf16[128,1024]{1,0:T(8,128)(2,1)S(1)}, u32[]{:S(2)}, u32[]{:S(2)}) collective-permute-start(bf16[128,1024]{1,0:T(8,128)(2,1)S(1)} %add_convert_fusion.3), channel_id=1, source_target_pairs={{1,0},{2,1},{3,2},{4,3},{5,4},{6,5},{7,6},{9,8},{10,9},{11,10},{12... | collective-permute-start | bytes 786440 | tf_op jit(solution)/shard_map/while/body/eval_jaxpr/ppermute | solution.py:12
  419.5 10.4 %collective-permute-start.1 = (bf16[128,1024]{1,0:T(8,128)(2,1)S(1)}, bf16[128,1024]{1,0:T(8,128)(2,1)S(1)}, u32[]{:S(2)}, u32[]{:S(2)}) collective-permute-start(bf16[128,1024]{1,0:T(8,128)(2,1)S(1)} %add_convert_fusion.3), channel_id=1, source_target_pairs={{1,0},{2,1},{3,2},{4,3},{5,4},{6,5},{7,6},{9,8},{10,9},{11,10},{12... | collective-permute-start | bytes 786440 | tf_op jit(solution)/shard_map/while/body/eval_jaxpr/ppermute | solution.py:12
  438.3 10.4 %collective-permute-start.1 = (bf16[128,1024]{1,0:T(8,128)(2,1)S(1)}, bf16[128,1024]{1,0:T(8,128)(2,1)S(1)}, u32[]{:S(2)}, u32[]{:S(2)}) collective-permute-start(bf16[128,1024]{1,0:T(8,128)(2,1)S(1)} %add_convert_fusion.3), channel_id=1, source_target_pairs={{1,0},{2,1},{3,2},{4,3},{5,4},{6,5},{7,6},{9,8},{10,9},{11,10},{12... | collective-permute-start | bytes 786440 | tf_op jit(solution)/shard_map/while/body/eval_jaxpr/ppermute | solution.py:12
  457.1 10.4 %collective-permute-start.1 = (bf16[128,1024]{1,0:T(8,128)(2,1)S(1)}, bf16[128,1024]{1,0:T(8,128)(2,1)S(1)}, u32[]{:S(2)}, u32[]{:S(2)}) collective-permute-start(bf16[128,1024]{1,0:T(8,128)(2,1)S(1)} %add_convert_fusion.3), channel_id=1, source_target_pairs={{1,0},{2,1},{3,2},{4,3},{5,4},{6,5},{7,6},{9,8},{10,9},{11,10},{12... | collective-permute-start | bytes 786440 | tf_op jit(solution)/shard_map/while/body/eval_jaxpr/ppermute | solution.py:12
  482.1 190.3 %reduce-scatter.8.cloned.1.call-start = ((), (), s32[]{:S(2)}) async-start(), calls=%async_computation.4 | async-start | bytes 1179648 | tf_op jit(solution)/shard_map/reduce_scatter | solution.py:109
  489.4 256.8 %reduce-scatter.12.cloned.1.call-start = ((), (), s32[]{:S(2)}) async-start(), calls=%async_computation.6 | async-start | bytes 2228224 | tf_op jit(solution)/shard_map/reduce_scatter | solution.py:124
  499.0 135.0 %copy-start.6 = (u32[128]{0:T(128)S(1)}, u32[128]{0:T(128)}, u32[]{:S(2)}) copy-start(u32[128]{0:T(128)} %constant.72) | copy-start | bytes 1540
  499.0 247.2 %copy-start.1 = (bf16[1,1024,1024]{2,1,0:T(8,128)(2,1)S(1)}, bf16[1,1024,1024]{2,1,0:T(8,128)(2,1)}, u32[]{:S(2)}) copy-start(bf16[1,1024,1024]{2,1,0:T(8,128)(2,1)} %param.14) | copy-start | bytes 6291460
  617.3 18.0 %collective-permute-start.3 = (bf16[1024,60]{0,1:T(8,128)(2,1)S(1)}, bf16[1024,60]{0,1:T(8,128)(2,1)S(1)}, u32[]{:S(2)}, u32[]{:S(2)}) collective-permute-start(bf16[1024,60]{0,1:T(8,128)(2,1)S(1)} %slice.3), channel_id=1, source_target_pairs={{0,8},{8,16},{16,24},{24,32},{32,40},{40,48},{48,56},{56,64},{64,7... | collective-permute-start | bytes 368648
  627.5 8.2 %collective-permute-start.2 = (bf16[1024,60]{0,1:T(8,128)(2,1)S(1)}, bf16[1024,60]{0,1:T(8,128)(2,1)}, u32[]{:S(2)}, u32[]{:S(2)}) collective-permute-start(bf16[1024,60]{0,1:T(8,128)(2,1)S(1)} %slice.2), channel_id=1, source_target_pairs={{0,8},{8,16},{16,24},{24,32},{32,40},{40,48},{48,56},{56,64},{64,7... | collective-permute-start | bytes 368648
  (7 other events, 264.8 us)
Sparse Core Ops, SparseCore 0:
  10.4 113.4 all-gather.6
  126.3 77.2 all-gather.4
  482.2 148.7 reduce-scatter.9
  633.8 38.5 reduce-scatter.7
  676.8 69.3 reduce-scatter.11
